TPU v7x, 128 devices: a whole 4x4x4 slice. The times are simulated.
128 devices in a mesh: ctx: 16 (over z_hi, x, core), head: 8 (over z_lo, y).
Axes of the slice: x: 4, y: 4, z: 4 (z_hi: 2, z_lo: 2; z = z_hi * 2 + z_lo), core: 2. Of those that a mesh axis runs over, the one named last changes fastest.
Arguments:
- tokens: bfloat16 [16384, 4096], P('ctx', 'head'), may hold values from -23 to 23
- proj_weight: bfloat16 [4096, 32, 384], P(None, 'head'), may hold values from -1 to 1
- partner_shard: int32 [32, 256, 3], P('head'), may hold values from 0 to 15, all different within a row; in each aligned block of 16 rows (0 to 15, 16 to 31, ..., all dimensions but the last counted through in order) at most 6 rows name the same one
- partner_block: int32 [32, 256, 3], P('head'), may hold values from 0 to 15
Outputs:
- attended: bfloat16 [16384, 32, 128], P('ctx', 'head')
Inputs may be any that keep to these rules, and one draw needn't show every extreme that they name: `partner_shard`: the 3 entries of one row differ. For each head, within each aligned run of 16 block rows, no value is named more than 6 times, and some runs name one value exactly 6 times.
All inputs are finite; a program needn't handle non-finite values.
Results may differ from a plain program's by a relative error of at most 0.008.
Values may be sent and summed in bfloat16 or wider, within the bound.
A program may use at most 192 MiB of HBM per device.

v0:
```python
import jax
import jax.numpy as jnp
from jax import lax
from jax.sharding import PartitionSpec as P

HEAD_DIMENSION = 128
BLK = 64
GLOB = 2
RAND = 3


def padded_2(cells, sides, width):
    for axis, dim in sides:
        count = lax.axis_size(axis)
        head = lax.slice_in_dim(cells, 0, width, axis=dim)
        tail = lax.slice_in_dim(cells, cells.shape[dim] - width, cells.shape[dim], axis=dim)
        cells = jnp.concatenate(
            [
                lax.ppermute(tail, axis, [(i, (i + 1) % count) for i in range(count)]),
                cells,
                lax.ppermute(head, axis, [((i + 1) % count, i) for i in range(count)]),
            ],
            axis=dim,
        )
    return cells


def from_root(block, axis, holder):
    block = jnp.where(lax.axis_index(axis) == holder, block, jnp.zeros_like(block))
    return lax.psum(block, axis)


def combined_all(part, axis, combine):
    gathered = jax.tree.map(lambda a: lax.all_gather(a, axis), part)

    def take(source):
        return jax.tree.map(lambda a: lax.dynamic_index_in_dim(a, source, 0, False), gathered)

    return lax.fori_loop(
        1, lax.axis_size(axis), lambda source, state: combine(state, take(source)), take(0)
    )


def per_device(tokens, proj_weight, partner_shard, partner_block):
    row_count = tokens.shape[0]
    head_count = proj_weight.shape[1]
    blocks = row_count // BLK
    shard_index = lax.axis_index("ctx")
    inverse_root_scale = HEAD_DIMENSION ** (-0.5)
    packed = jnp.einsum(
        "td,dhe->the",
        lax.all_gather(tokens, "head", axis=1, tiled=True),
        proj_weight,
        preferred_element_type=jnp.float32,
    ).astype(jnp.bfloat16)
    queries = packed[..., :HEAD_DIMENSION]
    keyval = packed[..., HEAD_DIMENSION:]
    padded = padded_2(keyval, (("ctx", 0),), BLK)
    window = jnp.concatenate(
        [
            padded[0:row_count].reshape(blocks, BLK, head_count, 2 * HEAD_DIMENSION),
            padded[BLK : row_count + BLK].reshape(blocks, BLK, head_count, 2 * HEAD_DIMENSION),
            padded[2 * BLK : row_count + 2 * BLK].reshape(
                blocks, BLK, head_count, 2 * HEAD_DIMENSION
            ),
        ],
        axis=1,
    )
    global_pack = from_root(packed[: GLOB * BLK], "ctx", 0)
    global_query = global_pack[..., :HEAD_DIMENSION]
    global_keyval = global_pack[..., HEAD_DIMENSION:]
    row_total = blocks * RAND
    owners = lax.dynamic_slice_in_dim(partner_shard, shard_index * blocks, blocks, 1).reshape(
        head_count, row_total
    )
    offsets = lax.dynamic_slice_in_dim(partner_block, shard_index * blocks, blocks, 1).reshape(
        head_count, row_total
    )
    partner_index = owners * blocks + offsets
    block_rows = lax.all_gather(keyval, "ctx", axis=0, tiled=True)
    piece_blocks = block_rows.shape[0] // BLK
    piece_hot = (partner_index[..., None] == jnp.arange(piece_blocks)).astype(jnp.bfloat16)
    blocked = block_rows.reshape(piece_blocks, BLK, head_count, 2 * HEAD_DIMENSION)
    fetched = jnp.einsum(
        "hrb,bthe->hrte", piece_hot, blocked, preferred_element_type=jnp.float32
    ).astype(jnp.bfloat16)
    remote = fetched
    remote = remote.reshape(head_count, blocks, RAND * BLK, 2 * HEAD_DIMENSION)
    blocked_query_rows = queries.reshape(blocks, BLK, head_count, HEAD_DIMENSION)
    window_scores = jnp.einsum(
        "bqhd,bkhd->bhqk",
        blocked_query_rows,
        window[..., :HEAD_DIMENSION],
        preferred_element_type=jnp.float32,
    )
    global_scores = jnp.einsum(
        "bqhd,khd->bhqk",
        blocked_query_rows,
        global_keyval[..., :HEAD_DIMENSION],
        preferred_element_type=jnp.float32,
    )
    remote_scores = jnp.einsum(
        "bqhd,hbkd->bhqk",
        blocked_query_rows,
        remote[..., :HEAD_DIMENSION],
        preferred_element_type=jnp.float32,
    )
    logit_scores = (
        jnp.concatenate([window_scores, global_scores, remote_scores], axis=-1) * inverse_root_scale
    )
    softmax_weight_matrix = jax.nn.softmax(logit_scores, axis=-1).astype(jnp.bfloat16)
    width_window = 3 * BLK
    width_global = GLOB * BLK
    context = jnp.einsum(
        "bhqk,bkhd->bqhd",
        softmax_weight_matrix[..., :width_window],
        window[..., HEAD_DIMENSION:],
        preferred_element_type=jnp.float32,
    )
    context = context + jnp.einsum(
        "bhqk,khd->bqhd",
        softmax_weight_matrix[..., width_window : width_window + width_global],
        global_keyval[..., HEAD_DIMENSION:],
        preferred_element_type=jnp.float32,
    )
    context = context + jnp.einsum(
        "bhqk,hbkd->bqhd",
        softmax_weight_matrix[..., width_window + width_global :],
        remote[..., HEAD_DIMENSION:],
        preferred_element_type=jnp.float32,
    )
    sparse_attention_output = context.astype(jnp.bfloat16).reshape(
        row_count, head_count, HEAD_DIMENSION
    )
    lead_scores = (
        jnp.einsum(
            "qhd,khd->hqk",
            global_query,
            keyval[..., :HEAD_DIMENSION],
            preferred_element_type=jnp.float32,
        )
        * inverse_root_scale
    )
    maxima = jnp.max(lead_scores, axis=-1)
    exp_terms = jnp.exp(lead_scores - maxima[..., None])
    totals = jnp.sum(exp_terms, axis=-1)
    summed = jnp.einsum(
        "hqk,khd->hqd",
        exp_terms,
        keyval[..., HEAD_DIMENSION:].astype(jnp.float32),
        precision=lax.Precision.HIGHEST,
    )

    def combine(first, second):
        max_first, total_first, sum_first = first
        max_second, total_second, sum_second = second
        larger = jnp.maximum(max_first, max_second)
        factor_first = jnp.exp(max_first - larger)
        factor_second = jnp.exp(max_second - larger)
        return (
            larger,
            total_first * factor_first + total_second * factor_second,
            sum_first * factor_first[..., None] + sum_second * factor_second[..., None],
        )

    maxima, totals, summed = combined_all((maxima, totals, summed), "ctx", combine)
    global_out = jnp.transpose((summed / totals[..., None]).astype(jnp.bfloat16), (1, 0, 2))
    head_rows = jnp.where(shard_index == 0, global_out, sparse_attention_output[: GLOB * BLK])
    return jnp.concatenate([head_rows, sparse_attention_output[GLOB * BLK :]], axis=0)


def solution(mesh):
    in_specs = (
        P("ctx", "head"),
        P(None, "head", None),
        P("head", None, None),
        P("head", None, None),
    )
    out_specs = P("ctx", "head", None)
    return jax.shard_map(
        per_device, mesh=mesh, in_specs=in_specs, out_specs=out_specs, check_vma=False
    )
```

profile of v0, /device:TPU:1, one launch (start us, length us, event | category | flops | bytes accessed | tf_op | source)
XLA Modules:
  0.0 600.8 jit_solution(12266525961735290425)
XLA Ops:
  6.5 0.7 all-gather.9.cloned.1.call-update
  7.3 0.0 all-reduce.2.cloned.1.call-start
  7.3 96.7 %all-gather.9.cloned.1.call-done = bf16[1024,4096]{1,0:T(8,128)(2,1)} async-done(((bf16[1024,512]{1,0:T(8,128)(2,1)}), bf16[1024,4096]{1,0:T(8,128)(2,1)}) %all-gather.9.cloned.1.call-update) | async-done | bytes 8388624 | tf_op jit(solution)/shard_map/all_gather | solution.py:52
  104.0 18.3 %fusion.22 = bf16[1024,4,384]{2,0,1:T(8,128)(2,1)S(1)} fusion(bf16[4096,4,384]{2,1,0:T(4,128)(2,1)} %param.7, bf16[1024,4096]{1,0:T(8,128)(2,1)} %all-gather.9.cloned.1.call-done), kind=kOutput, calls=%fused_computation.29 | convolution fusion | flops 12886474752 | bytes 24117248 | tf_op jit(solution)/shard_map/td,dhe->the/dot_general | solution.py:50
  122.3 0.8 slice_select_fusion
  123.2 0.0 all-reduce.2.cloned.1.call-update
  123.2 0.0 all-gather.13.cloned.1.call-start
  123.2 138.2 %all-reduce.2.cloned.1.call-done = bf16[128,4,384]{2,0,1:T(8,128)(2,1)} async-done(((bf16[128,4,384]{2,0,1:T(8,128)(2,1)}), bf16[128,4,384]{2,0,1:T(8,128)(2,1)}) %all-reduce.2.cloned.1.call-update) | async-done | bytes 393232 | tf_op jit(solution)/shard_map/psum | solution.py:30
  261.4 1.4 multiply_reduce_fusion
  262.8 1.3 copy-done.1
  264.1 2.2 fusion.30
  266.3 0.0 all-gather.13.cloned.1.call-update
  266.3 0.0 all-gather.11.cloned.1.call-start
  266.4 1.5 slice.118
  267.9 0.0 all-gather.11.cloned.1.call-update
  267.9 1.8 fusion.56
  269.7 0.7 collective-permute-start.1
  270.4 0.8 dynamic-slice_add_fusion
  271.1 0.1 copy.40
  271.2 0.1 add.84
  271.3 1.3 slice.116
  272.6 1.4 collective-permute-done.1
  274.1 0.3 pad_maximum_fusion.2
  274.4 5.0 pad_maximum_fusion
  279.4 3.4 fusion.54
  282.8 4.1 fusion.20
  286.9 25.5 %all-gather.3 = f32[16,4,128]{2,1,0:T(4,128)S(1)} all-gather(f32[1,4,128]{2,1,0:T(4,128)S(1)} %bitcast.75), channel_id=2, replica_groups=mesh['ctx'=16,'head'=8] {'ctx'}, dimensions={0}, use_global_device_ids=true | all-gather | bytes 34816 | tf_op jit(solution)/shard_map/all_gather | solution.py:34
  312.4 0.5 fusion.31
  312.9 19.5 %all-gather.4 = f32[16,4,128]{2,1,0:T(4,128)S(1)} all-gather(f32[1,4,128]{2,1,0:T(4,128)S(1)} %bitcast.76), channel_id=3, replica_groups=mesh['ctx'=16,'head'=8] {'ctx'}, dimensions={0}, use_global_device_ids=true | all-gather | bytes 34816 | tf_op jit(solution)/shard_map/all_gather | solution.py:34
  332.4 1.3 convolution_bitcast_fusion
  333.7 0.0 all-gather.13.cloned.1.call-done
  333.8 1.0 slice.115
  334.8 19.0 %while.19 = (s32[]{:T(128)}, f32[4,128]{1,0:T(4,128)S(1)}, f32[4,128]{1,0:T(4,128)S(1)}, f32[4,128,128]{2,1,0:T(8,128)S(1)}, f32[16,4,128]{2,1,0:T(4,128)S(1)}, ...) while((s32[]{:T(128)}, f32[4,128]{1,0:T(4,128)S(1)}, ...), condition=%wide.region_4.5_spmd, body=%wide.region_3.4_spmd.sunk | while | flops 199685 | bytes 807063 | solution.py:39
  334.8 1.3 fusion.61
  336.1 1.2 fusion.61
  337.4 1.2 fusion.61
  338.7 1.3 fusion.61
  340.0 1.2 fusion.61
  341.2 1.2 fusion.61
  342.5 1.2 fusion.61
  343.8 1.2 fusion.61
  345.0 1.2 fusion.61
  346.3 1.2 fusion.61
  347.5 1.2 fusion.61
  348.8 1.2 fusion.61
  350.1 1.2 fusion.61
  351.3 1.2 fusion.61
  352.6 1.2 fusion.61
  353.8 158.4 %all-gather.11.cloned.1.call-done = bf16[16384,4,256]{2,0,1:T(8,128)(2,1)} async-done(((bf16[1024,4,256]{2,0,1:T(8,128)(2,1)}), bf16[16384,4,256]{2,0,1:T(8,128)(2,1)}) %all-gather.11.cloned.1.call-update) | async-done | bytes 33554448 | tf_op jit(solution)/shard_map/all_gather | solution.py:80
  512.2 34.4 %fusion.11 = bf16[4,48,64,256]{3,1,2,0:T(8,128)(2,1)S(1)} fusion(bf16[256,64,4,256]{3,1,0,2:T(8,128)(2,1)} %bitcast.65, s32[4,48]{1,0:T(4,128)S(1)} %add.84), kind=kOutput, calls=%fused_computation.20 | convolution fusion | flops 1613807616 | bytes 39846656 | tf_op jit(solution)/shard_map/hrb,bthe->hrte/dot_general | solution.py:84
  546.6 2.5 copy.42
  549.1 1.8 fusion.55
  550.9 4.1 fusion.18
  555.0 28.1 %fusion.57 = (f32[16,4,64]{2,1,0:T(4,128)S(1)}, f32[16,4,64,512]{3,2,1,0:T(8,128)}) fusion(f32[16,4,64,192]{3,2,1,0:T(8,128)} %fusion.18, f32[16,4,64,128]{3,2,1,0:T(8,128)S(1)} %convolution_bitcast_fusion, f32[16,4,64,192]{3,2,1,0:T(8,128)S(1)} %copy-done.5), kind=kOutput, calls=%fused_computation.71 | output fusion | flops 10486271 | bytes 16793600 | tf_op jit(solution)/shard_map/sub | solution.py:111
  583.1 4.1 divide_convert_fusion
  587.1 1.3 fusion.14
  588.4 1.6 fusion.36
  590.0 0.4 copy-done.3
  590.4 1.4 fusion.29
  591.8 0.1 slice.130
  591.9 0.1 copy.47
  592.0 0.1 bitcast_select_fusion
  592.1 0.1 pad_maximum_fusion.3
  592.2 1.8 copy.48
  (32 shorter events, 0.4 us)
Async XLA Ops:
  6.5 97.4 %all-gather.9.cloned.1.call-start = ((), (), s32[]{:S(2)}) async-start(), calls=%async_computation | async-start | bytes 9437184 | tf_op jit(solution)/shard_map/all_gather | solution.py:52
  7.3 254.2 %all-reduce.2.cloned.1.call-start = ((), (), s32[]{:S(2)}) async-start(), calls=%async_computation.1 | async-start | bytes 786432 | tf_op jit(solution)/shard_map/psum | solution.py:30
  122.3 144.1 %copy-start.4 = (bf16[1024,4,384]{2,0,1:T(8,128)(2,1)}, bf16[1024,4,384]{2,0,1:T(8,128)(2,1)S(1)}, u32[]{:S(2)}) copy-start(bf16[1024,4,384]{2,0,1:T(8,128)(2,1)S(1)} %fusion.22) | copy-start | bytes 9437188
  123.2 210.6 %all-gather.13.cloned.1.call-start = ((), (), s32[]{:S(2)}) async-start(), calls=%async_computation.3 | async-start | bytes 4456448 | tf_op jit(solution)/shard_map/all_gather | solution.py:34
  262.8 1.3 copy-start.1
  266.3 245.9 %all-gather.11.cloned.1.call-start = ((), (), s32[]{:S(2)}) async-start(), calls=%async_computation.2 | async-start | bytes 35651584 | tf_op jit(solution)/shard_map/all_gather | solution.py:80
  267.9 6.2 %copy-start = (bf16[1024,4,256]{2,0,1:T(8,128)(2,1)S(1)}, bf16[1024,4,256]{2,0,1:T(8,128)(2,1)}, u32[]{:S(2)}) copy-start(bf16[1024,4,256]{2,0,1:T(8,128)(2,1)} %slice.118) | copy-start | bytes 6291460
  269.7 2.9 collective-permute-start
  269.7 4.4 collective-permute-start.1
  282.8 29.6 %copy-start.2 = (f32[4,128,1024]{2,1,0:T(8,128)S(1)}, f32[4,128,1024]{2,1,0:T(8,128)}, u32[]{:S(2)}) copy-start(f32[4,128,1024]{2,1,0:T(8,128)} %copy-done.1) | copy-start | bytes 6291460
  550.9 4.1 copy-start.5
  588.4 2.0 copy-start.3
Sparse Core Ops, SparseCore 0:
  9.0 94.9 all-gather.8
  123.3 138.0 all-reduce.1
  266.4 57.4 all-gather.12
  326.3 185.8 all-gather.10
where the time goes:
time: 610 us; the launch traced here: 601 us
  waiting for transfers between devices  396 us (65%)
  matrix products  70 us (11%)
  other arithmetic  58.3 us (10%)
  blocking collectives  45 us (7%)
  local copies, waits for them, and re-layouts  17.1 us (3%)
  between operations  13.6 us (2%)
    all_gather x1, waiting for transfers between devices, per_device(): block_rows = lax.all_gather(keyval, 'ctx', axis=0, tiled=True)  158 us
    psum x1, waiting for transfers between devices, from_root(): return lax.psum(block, axis)  138 us
    all_gather x1, waiting for transfers between devices, per_device(): lax.all_gather(tokens, 'head', axis=1, tiled=True)  96.7 us
    all_gather x2, blocking collectives, combined_all(): gathered = jax.tree.map(lambda a: lax.all_gather(a, axis), part)  45 us
    dot_general x1, matrix products, per_device(): jnp.einsum('hrb,bthe->hrte', piece_hot, blocked, preferred_element_type=j...  34.4 us
    sub x1, other arithmetic, per_device(): jax.nn.softmax(logit_scores, axis=-1).astype(jnp.bfloat16)  28.1 us
    dot_general x1, matrix products, per_device(): jnp.einsum('td,dhe->the', lax.all_gather(tokens, 'head', axis=1, tiled=Tr...  18.3 us
    add x15, other arithmetic, combine(): sum_first * factor_first[..., None] + sum_second * factor_second[..., None]  18.2 us
  transfers between devices with their start and end apart: 6, of which 4 were waited for; matrix products, arithmetic and copies ran while one was open for 7% of the time, Pallas kernels for 0%

commit v1 on v0

--- a/solution.py
+++ b/solution.py
@@ -7,6 +7,9 @@
 BLK = 64
 GLOB = 2
 RAND = 3
+set_array_up = lambda here_x, where_dim: jnp.concatenate(
+    lax.all_to_all(jnp.stack(lax.psum(1, "ctx") * [here_x]), "ctx", 0, 0), axis=where_dim
+)
 
 
 def padded_2(cells, sides, width):
@@ -77,7 +80,7 @@
         head_count, row_total
     )
     partner_index = owners * blocks + offsets
-    block_rows = lax.all_gather(keyval, "ctx", axis=0, tiled=True)
+    block_rows = set_array_up(keyval, 0)
     piece_blocks = block_rows.shape[0] // BLK
     piece_hot = (partner_index[..., None] == jnp.arange(piece_blocks)).astype(jnp.bfloat16)
     blocked = block_rows.reshape(piece_blocks, BLK, head_count, 2 * HEAD_DIMENSION)

time: 610 us -> 799 us (1.31)
  waiting for transfers between devices: 396 us -> 546 us
  local copies, waits for them, and re-layouts: 17.1 us -> 51.4 us
    ppermute x1, waiting for transfers between devices: 0.01 us -> 171 us  [padded_2(): lax.ppermute(tail, axis, [(i, (i + 1) % count) for i in range(count)])]
    all_gather x1 -> x0, waiting for transfers between devices: 158 us -> none  [per_device(): block_rows = lax.all_gather(keyval, 'ctx', axis=0, tiled=True)]
    psum x1, waiting for transfers between devices: 138 us -> 278 us  [from_root(): return lax.psum(block, axis)]
    all_to_all x0 -> x1, local copies, waits for them, and re-layouts: none -> 22.9 us  [lax.all_to_all(jnp.stack(lax.psum(1, 'ctx') * [here_x]), 'ctx', 0, 0)]
    another operation x0 -> x1, local copies, waits for them, and re-layouts: none -> 11 us  [jnp.stack(lax.psum(1, 'ctx') * [here_x])]
  transfers between devices with their start and end apart: 6 -> 6, of which waited for: 4 -> 3; matrix products, arithmetic and copies ran while one was open for 7% -> 6% of each run, Pallas kernels for 0% -> 0%
where the time goes in v1:
time: 799 us; the launch traced here: 793 us
  waiting for transfers between devices  546 us (68%)
  matrix products  71.7 us (9%)
  other arithmetic  58.5 us (7%)
  local copies, waits for them, and re-layouts  51.4 us (6%)
  blocking collectives  42.3 us (5%)
  between operations  13.6 us (2%)
  starting transfers between devices  8.42 us (1%)
    psum x1, waiting for transfers between devices, from_root(): return lax.psum(block, axis)  278 us
    ppermute x1, waiting for transfers between devices, padded_2(): lax.ppermute(tail, axis, [(i, (i + 1) % count) for i in range(count)])  171 us
    all_gather x1, waiting for transfers between devices, per_device(): lax.all_gather(tokens, 'head', axis=1, tiled=True)  96.7 us
    all_gather x2, blocking collectives, combined_all(): gathered = jax.tree.map(lambda a: lax.all_gather(a, axis), part)  42.3 us
    dot_general x1, matrix products, per_device(): jnp.einsum('hrb,bthe->hrte', piece_hot, blocked, preferred_element_type=j...  34.4 us
    sub x1, other arithmetic, per_device(): jax.nn.softmax(logit_scores, axis=-1).astype(jnp.bfloat16)  28.1 us
    all_to_all x1, local copies, waits for them, and re-layouts, lax.all_to_all(jnp.stack(lax.psum(1, 'ctx') * [here_x]), 'ctx', 0, 0)  22.9 us
    dot_general x1, matrix products, per_device(): jnp.einsum('td,dhe->the', lax.all_gather(tokens, 'head', axis=1, tiled=Tr...  18.3 us
  transfers between devices with their start and end apart: 6, of which 3 were waited for; matrix products, arithmetic and copies ran while one was open for 6% of the time, Pallas kernels for 0%

profile of v1, /device:TPU:1, one launch (start us, length us, event | category | flops | bytes accessed | tf_op | source)
XLA Modules:
  0.0 792.7 jit_solution(3771661223384916965)
XLA Ops:
  6.5 0.7 all-gather.8.cloned.1.call-update
  7.3 96.7 %all-gather.8.cloned.1.call-done = bf16[1024,4096]{1,0:T(8,128)(2,1)} async-done(((bf16[1024,512]{1,0:T(8,128)(2,1)}), bf16[1024,4096]{1,0:T(8,128)(2,1)}) %all-gather.8.cloned.1.call-update) | async-done | bytes 8388624 | tf_op jit(solution)/shard_map/all_gather | solution.py:55
  104.0 18.3 %fusion.22 = bf16[1024,4,384]{2,0,1:T(8,128)(2,1)S(1)} fusion(bf16[4096,4,384]{2,1,0:T(4,128)(2,1)} %param.7, bf16[1024,4096]{1,0:T(8,128)(2,1)} %all-gather.8.cloned.1.call-done), kind=kOutput, calls=%fused_computation.29 | convolution fusion | flops 12886474752 | bytes 24117248 | tf_op jit(solution)/shard_map/td,dhe->the/dot_general | solution.py:53
  122.3 1.7 copy-done.3
  124.0 0.1 slice.118
  124.1 11.0 %stack.2 = bf16[16,1024,4,256]{3,1,2,0:T(8,128)(2,1)} broadcast(bf16[1024,4,256]{2,0,1:T(8,128)(2,1)S(1)} %slice.118), dimensions={1,2,3} | broadcast | bytes 35651584 | tf_op jit(solution)/shard_map/stack | solution.py:11
  135.1 7.4 all-to-all-start
  142.5 0.0 all-reduce.2.cloned.1.call-start
  142.6 1.8 slice_select_fusion
  144.4 0.0 all-gather.10.cloned.1.call-start
  144.5 277.9 %all-reduce.2.cloned.1.call-done = bf16[128,4,384]{2,0,1:T(8,128)(2,1)} async-done(((bf16[128,4,384]{2,0,1:T(8,128)(2,1)}), bf16[128,4,384]{2,0,1:T(8,128)(2,1)}) %all-reduce.2.cloned.1.call-update) | async-done | bytes 393232 | tf_op jit(solution)/shard_map/psum | solution.py:33
  422.3 1.8 multiply_reduce_fusion
  424.2 1.5 copy-done
  425.7 3.4 fusion.30
  429.1 1.6 fusion.56
  430.7 0.7 collective-permute-start
  431.4 0.3 collective-permute-start.1
  431.7 0.1 dynamic-slice_add_fusion
  431.8 0.1 copy.40
  431.9 0.1 add.84
  432.0 1.3 slice.116
  433.3 171.1 %collective-permute-done = bf16[64,4,256]{2,0,1:T(8,128)(2,1)S(1)} collective-permute-done((bf16[64,4,256]{2,0,1:T(8,128)(2,1)}, bf16[64,4,256]{2,0,1:T(8,128)(2,1)S(1)}, u32[]{:S(2)}, u32[]{:S(2)}) %collective-permute-start) | collective-permute-done | bytes 131104 | tf_op jit(solution)/shard_map/ppermute | solution.py:22
  604.4 0.3 pad_maximum_fusion.2
  604.7 5.0 pad_maximum_fusion
  609.7 3.4 fusion.54
  613.1 4.1 fusion.20
  617.2 22.4 %all-gather.3 = f32[16,4,128]{2,1,0:T(4,128)S(1)} all-gather(f32[1,4,128]{2,1,0:T(4,128)S(1)} %bitcast.75), channel_id=2, replica_groups=mesh['ctx'=16,'head'=8] {'ctx'}, dimensions={0}, use_global_device_ids=true | all-gather | bytes 34816 | tf_op jit(solution)/shard_map/all_gather | solution.py:37
  639.7 0.5 fusion.31
  640.2 19.9 %all-gather.4 = f32[16,4,128]{2,1,0:T(4,128)S(1)} all-gather(f32[1,4,128]{2,1,0:T(4,128)S(1)} %bitcast.76), channel_id=3, replica_groups=mesh['ctx'=16,'head'=8] {'ctx'}, dimensions={0}, use_global_device_ids=true | all-gather | bytes 34816 | tf_op jit(solution)/shard_map/all_gather | solution.py:37
  660.0 1.3 convolution_bitcast_fusion
  661.4 0.0 all-gather.10.cloned.1.call-done
  661.4 1.0 slice.115
  662.4 18.9 %while.19 = (s32[]{:T(128)}, f32[4,128]{1,0:T(4,128)S(1)}, f32[4,128]{1,0:T(4,128)S(1)}, f32[4,128,128]{2,1,0:T(8,128)S(1)}, f32[16,4,128]{2,1,0:T(4,128)S(1)}, ...) while((s32[]{:T(128)}, f32[4,128]{1,0:T(4,128)S(1)}, ...), condition=%wide.region_4.5_spmd, body=%wide.region_3.4_spmd.sunk | while | flops 199685 | bytes 807063 | solution.py:42
  662.4 1.2 fusion.61
  663.7 1.2 fusion.61
  664.9 1.2 fusion.61
  666.2 1.2 fusion.61
  667.5 1.2 fusion.61
  668.7 1.2 fusion.61
  670.0 1.2 fusion.61
  671.2 1.2 fusion.61
  672.5 1.2 fusion.61
  673.7 1.2 fusion.61
  675.0 1.2 fusion.61
  676.3 1.2 fusion.61
  677.5 1.2 fusion.61
  678.8 1.2 fusion.61
  680.0 1.2 fusion.61
  681.3 22.9 %copy.41 = bf16[16,1024,4,256]{3,1,0,2:T(8,128)(2,1)} copy(bf16[16,1024,4,256]{3,1,2,0:T(8,128)(2,1)} %all-to-all-done) | data formatting | bytes 67108864 | tf_op jit(solution)/shard_map/all_to_all | solution.py:11
  704.2 34.4 %fusion.11 = bf16[4,48,64,256]{3,1,2,0:T(8,128)(2,1)S(1)} fusion(bf16[256,64,4,256]{3,1,0,2:T(8,128)(2,1)} %bitcast.65, s32[4,48]{1,0:T(4,128)S(1)} %add.84), kind=kOutput, calls=%fused_computation.20 | convolution fusion | flops 1613807616 | bytes 39846656 | tf_op jit(solution)/shard_map/hrb,bthe->hrte/dot_general | solution.py:87
  738.5 2.5 copy.43
  741.0 1.8 fusion.55
  742.8 4.1 fusion.18
  746.9 28.1 %fusion.57 = (f32[16,4,64]{2,1,0:T(4,128)S(1)}, f32[16,4,64,512]{3,2,1,0:T(8,128)}) fusion(f32[16,4,64,192]{3,2,1,0:T(8,128)} %fusion.18, f32[16,4,64,128]{3,2,1,0:T(8,128)S(1)} %convolution_bitcast_fusion, f32[16,4,64,192]{3,2,1,0:T(8,128)S(1)} %copy-done.4), kind=kOutput, calls=%fused_computation.71 | output fusion | flops 10486271 | bytes 16793600 | tf_op jit(solution)/shard_map/sub | solution.py:114
  775.0 4.1 divide_convert_fusion
  779.0 1.3 fusion.14
  780.3 1.6 fusion.36
  781.9 0.4 copy-done.2
  782.3 1.4 fusion.29
  783.7 0.1 slice.130
  783.8 0.1 copy.48
  783.9 0.1 bitcast_select_fusion
  784.1 0.1 pad_maximum_fusion.3
  784.1 1.8 copy.49
  (35 shorter events, 0.5 us)
Async XLA Ops:
  6.5 97.4 %all-gather.8.cloned.1.call-start = ((), (), s32[]{:S(2)}) async-start(), calls=%async_computation.1 | async-start | bytes 9437184 | tf_op jit(solution)/shard_map/all_gather | solution.py:55
  122.3 1.7 copy-start.3
  135.1 546.1 %all-to-all-start = ((bf16[16,1024,4,256]{3,1,2,0:T(8,128)(2,1)}), bf16[16,1024,4,256]{3,1,2,0:T(8,128)(2,1)}, u32[]{:S(2)}, u32[]{:S(2)}) async-start(bf16[16,1024,4,256]{3,1,2,0:T(8,128)(2,1)} %stack.2), calls=%async_computation | async-start | bytes 67108864 | tf_op jit(solution)/shard_map/all_to_all | solution.py:11
  142.5 279.8 %all-reduce.2.cloned.1.call-start = ((), (), s32[]{:S(2)}) async-start(), calls=%async_computation.2 | async-start | bytes 786432 | tf_op jit(solution)/shard_map/psum | solution.py:33
  144.4 287.3 %copy-start.5 = (s32[4,256,3]{1,0,2:T(4,128)S(1)}, s32[4,256,3]{1,0,2:T(4,128)}, u32[]{:S(2)}) copy-start(s32[4,256,3]{1,0,2:T(4,128)} %param.9) | copy-start | bytes 36868
  144.4 287.3 %copy-start.6 = (s32[4,256,3]{1,0,2:T(4,128)S(1)}, s32[4,256,3]{1,0,2:T(4,128)}, u32[]{:S(2)}) copy-start(s32[4,256,3]{1,0,2:T(4,128)} %param.8) | copy-start | bytes 36868
  144.4 517.0 %all-gather.10.cloned.1.call-start = ((), (), s32[]{:S(2)}) async-start(), calls=%async_computation.3 | async-start | bytes 4456448 | tf_op jit(solution)/shard_map/all_gather | solution.py:37
  424.2 1.5 copy-start
  430.7 173.7 %collective-permute-start = (bf16[64,4,256]{2,0,1:T(8,128)(2,1)}, bf16[64,4,256]{2,0,1:T(8,128)(2,1)S(1)}, u32[]{:S(2)}, u32[]{:S(2)}) collective-permute-start(bf16[64,4,256]{2,0,1:T(8,128)(2,1)} %get-tuple-element.206), channel_id=1, source_target_pairs={{0,8},{8,16},{16,24},{24,32},{32,40},{40,48},{48,56},{56,64},{64,7... | collective-permute-start | bytes 393224 | tf_op jit(solution)/shard_map/ppermute | solution.py:22
  431.4 173.0 %collective-permute-start.1 = (bf16[64,4,256]{2,0,1:T(8,128)(2,1)S(1)}, bf16[64,4,256]{2,0,1:T(8,128)(2,1)S(1)}, u32[]{:S(2)}, u32[]{:S(2)}) collective-permute-start(bf16[64,4,256]{2,0,1:T(8,128)(2,1)S(1)} %get-tuple-element.207), channel_id=1, source_target_pairs={{8,0},{16,8},{24,16},{32,24},{40,32},{48,40},{56,48},{64,56},{72,6... | collective-permute-start | bytes 393224 | tf_op jit(solution)/shard_map/ppermute | solution.py:24
  613.1 26.5 %copy-start.1 = (f32[4,128,1024]{2,1,0:T(8,128)S(1)}, f32[4,128,1024]{2,1,0:T(8,128)}, u32[]{:S(2)}) copy-start(f32[4,128,1024]{2,1,0:T(8,128)} %copy-done) | copy-start | bytes 6291460
  742.8 4.1 copy-start.4
  780.3 2.0 copy-start.2
Sparse Core Ops, SparseCore 0:
  9.0 94.9 all-gather.7
  145.8 276.4 all-reduce.1
  429.2 158.1 all-gather.9
